TPU v7x, 256 devices: a whole 4x4x8 slice. The times are simulated.
256 devices in a mesh: dp: 8 (over z), pipe: 4 (over y), seq: 8 (over x, core).
Axes of the slice: x: 4, y: 4, z: 8, core: 2. Of those that a mesh axis runs over, the one named last changes fastest.
Arguments:
- section_input: bfloat16 [4, 8, 1024, 1024], P('pipe', 'dp', 'seq'), may hold values from -6 to 6
- event_ids: int32 [8, 1024], P('dp', 'seq'), may hold values from 0 to 63
- lengths: int32 [8], P('dp'), may hold values from 256 to 1024, as said below
- clicks: int32 [8, 1024], P('dp', 'seq'), may hold values 0 or 1
- conversions: int32 [8, 1024], P('dp', 'seq'), may hold values 0 or 1
- conv_weight: bfloat16 [4, 3072, 1024], P('pipe'), may hold values from -0.109375 to 0.109375
- type_table: bfloat16 [4, 64, 1024], P('pipe'), may hold values from -3 to 3
- head_weight: bfloat16 [2, 1024], replicated, may hold values from -0.375 to 0.375
Outputs:
- conv_grad: float32 [4, 3072, 1024], P('pipe', ('dp', 'seq'))
- type_grad: float32 [4, 64, 1024], P('pipe', ('dp', 'seq'))
- input_grad: bfloat16 [4, 8, 1024, 1024], P('pipe', 'dp', 'seq')
Inputs may be any that keep to these rules, and one draw needn't show every extreme that they name: `lengths`: some history has all 1024 events real.
All inputs are finite; a program needn't handle non-finite values. No bound on the sum of `clicks` or of `conversions` on one device may be relied on, other than what follows from the above.
Results may differ from a plain program's by a relative error of at most 0.013.
Values may be sent and summed in bfloat16 or wider, within the bound.
No kernel may reach another device: no remote copies, remote signals or barrier semaphores. Data moves between devices by JAX's collectives and lax.ppermute only.
A program may use at most 256 MiB of HBM per device.

v0:
```python
import jax
import jax.numpy as jnp
from jax import lax
from jax.sharding import PartitionSpec as P

KERNEL = 3


EPS = 1e-06


def from_behind(array, axis, by):
    count = lax.axis_size(axis)
    pairs = [(i, i + by) for i in range(count) if 0 <= i + by < count]
    return lax.ppermute(array, axis, pairs)


def head_grad(out_bf, head_weight, click, convert, valid):
    logits = jnp.dot(out_bf, head_weight.T, preferred_element_type=jnp.float32)
    label_y = click.astype(jnp.float32)
    label_z = label_y * convert.astype(jnp.float32)
    weight_m = valid.astype(jnp.float32)

    def event_loss(first, second):
        soft = jax.nn.softplus
        rest = jnp.log(jax.nn.sigmoid(-first) + jax.nn.sigmoid(first) * jax.nn.sigmoid(-second))
        return (
            label_y * soft(-first)
            + (1.0 - label_y) * soft(first)
            + label_z * (soft(-first) + soft(-second))
            - (1.0 - label_z) * rest
        )

    _, pull = jax.vjp(event_loss, logits[:, 0], logits[:, 1])
    grad_first, grad_second = pull(weight_m)
    grad_logits = jnp.stack([grad_first, grad_second], axis=1)
    return jnp.dot(grad_logits, head_weight.astype(jnp.float32), precision=lax.Precision.HIGHEST)


def on_device(
    section_input, event_ids, lengths, clicks, conversions, conv_weight, type_table, head_weight
):
    inputs_bf = section_input[0, 0]
    rows, width = inputs_bf.shape
    halo_rows = rows // 2
    weight = conv_weight[0]
    table = type_table[0]
    kinds = table.shape[0]
    section = lax.axis_index("pipe")
    sections = lax.axis_size("pipe")
    spacing = jnp.right_shift(jnp.int32(rows // 4), section)
    inputs = inputs_bf.astype(jnp.float32)
    inv_rms = lax.rsqrt(jnp.mean(inputs * inputs, axis=-1, keepdims=True) + EPS)
    normed = inputs * inv_rms
    normed_bf = normed.astype(jnp.bfloat16)
    earlier = from_behind(normed_bf[rows - halo_rows :], "seq", 1)
    extended = jnp.concatenate([earlier, normed_bf], axis=0)
    taps = jnp.concatenate(
        [
            lax.dynamic_slice_in_dim(extended, halo_rows - tap * spacing, rows, 0)
            for tap in range(KERNEL)
        ],
        axis=1,
    )
    onehot = (event_ids[0][:, None] == jnp.arange(kinds, dtype=jnp.int32)[None, :]).astype(
        jnp.bfloat16
    )
    position = lax.axis_index("seq") * rows + jnp.arange(rows, dtype=jnp.int32)
    valid = position < lengths[0]
    is_last = section == sections - 1

    def forward_and_head():
        pre = jnp.dot(taps, weight, preferred_element_type=jnp.float32) + jnp.dot(
            onehot, table, preferred_element_type=jnp.float32
        )
        out_bf = (inputs + jax.nn.gelu(pre)).astype(jnp.bfloat16)
        return (pre, head_grad(out_bf, head_weight, clicks[0], conversions[0], valid))

    def active_work(incoming):
        pre, top_grad = forward_and_head()
        grad_out = jnp.where(is_last, top_grad, incoming)
        _, pull = jax.vjp(jax.nn.gelu, pre)
        grad_pre = pull(grad_out)[0].astype(jnp.bfloat16)
        conv_part = lax.dot_general(
            taps, grad_pre, (((0,), (0,)), ((), ())), preferred_element_type=jnp.float32
        )
        type_part = lax.dot_general(
            onehot, grad_pre, (((0,), (0,)), ((), ())), preferred_element_type=jnp.float32
        )
        grad_taps = lax.dot_general(
            grad_pre, weight, (((1,), (1,)), ((), ())), preferred_element_type=jnp.float32
        )
        grad_ext = jnp.zeros((halo_rows + rows, width), jnp.float32)
        for tap in range(KERNEL):
            start = halo_rows - tap * spacing
            current = lax.dynamic_slice_in_dim(grad_ext, start, rows, 0)
            grad_ext = lax.dynamic_update_slice_in_dim(
                grad_ext, current + grad_taps[:, tap * width : (tap + 1) * width], start, 0
            )
        return (conv_part, type_part, grad_ext, grad_out)

    def spare_work(incoming):
        return (
            jnp.zeros((KERNEL * width, width), jnp.float32),
            jnp.zeros((kinds, width), jnp.float32),
            jnp.zeros((halo_rows + rows, width), jnp.float32),
            jnp.zeros((rows, width), jnp.float32),
        )

    incoming = jnp.zeros((rows, width), jnp.float32)
    input_grad = jnp.zeros((rows, width), jnp.bfloat16)
    conv_total = jnp.zeros((KERNEL * width, width), jnp.float32)
    type_total = jnp.zeros((kinds, width), jnp.float32)
    for tick in range(sections):
        active = section == sections - 1 - tick
        reach = 2 * (rows // 4 >> sections - 1 - tick)
        conv_part, type_part, grad_ext, grad_out = lax.cond(
            active, active_work, spare_work, incoming
        )
        later = from_behind(
            grad_ext[halo_rows - reach : halo_rows].astype(jnp.bfloat16), "seq", -1
        ).astype(jnp.float32)
        grad_normed = grad_ext[halo_rows:] + jnp.concatenate(
            [jnp.zeros((rows - reach, width), jnp.float32), later], axis=0
        )
        inner = jnp.mean(grad_normed * normed, axis=-1, keepdims=True)
        grad_in = (grad_out + inv_rms * (grad_normed - normed * inner)).astype(jnp.bfloat16)
        input_grad = jnp.where(active, grad_in, input_grad)
        conv_total = conv_total + conv_part
        type_total = type_total + type_part
        if tick + 1 < sections:
            incoming = from_behind(grad_in, "pipe", -1).astype(jnp.float32)
    conv_share, type_share = (
        lax.psum_scatter(conv_total, ("dp", "seq"), scatter_dimension=0, tiled=True),
        lax.psum_scatter(type_total, ("dp", "seq"), scatter_dimension=0, tiled=True),
    )
    return (conv_share[None], type_share[None], input_grad[None, None])


def solution(mesh):
    placed = (
        P("pipe", "dp", "seq", None),
        P("dp", "seq"),
        P("dp"),
        P("dp", "seq"),
        P("dp", "seq"),
        P("pipe", None, None),
        P("pipe", None, None),
        P(),
    )
    return jax.shard_map(
        on_device,
        mesh=mesh,
        in_specs=placed,
        out_specs=(
            P("pipe", ("dp", "seq"), None),
            P("pipe", ("dp", "seq"), None),
            P("pipe", "dp", "seq", None),
        ),
        check_vma=False,
    )
```

profile of v0, /device:TPU:8, one launch (start us, length us, event | category | flops | bytes accessed | tf_op | source)
XLA Modules:
  0.0 562.4 jit_solution(1772185149322781711)
XLA Ops:
  7.2 1.1 multiply_reduce_fusion.4
  8.3 1.1 multiply_convert_fusion
  9.4 1.7 collective-permute-start
  11.1 1.0 bitcast_convert_fusion
  14.1 7.2 %conditional.4 = (f32[64,1024]{1,0:T(8,128)S(1)}, f32[192,1024]{1,0:T(8,128)}, f32[128,1024]{1,0:T(8,128)S(1)}, f32[3072,1024]{1,0:T(8,128)}) conditional(s32[]{:T(128)} %convert_element_type.141, () %tuple.40, (pred[]{:T(512)}, s32[1,128]{1,0:T(1,128)}, s32[1,128]{1,0:T(1,128)}, pred[128]{0:T(512)(128)(4,1)S(1)}, bf16[128,3072]{1,0:T(8,128)(2,1)S(1)}, ...), branch_computations={%region_1.0_spmd, %region_2.3_spmd} | conditional | flops 2457610496 | bytes 87754192 | solution.py:117
  14.1 6.2 %broadcast.198.clone = f32[3072,1024]{1,0:T(8,128)} broadcast(f32[]{:T(128)} %constant.115.clone), dimensions={} | broadcast | bytes 12582916 | tf_op jit(solution)/shard_map/broadcast.9
  22.1 1.3 collective-permute-start.1
  23.4 3.0 collective-permute-done.1
  26.4 1.3 multiply_reduce_fusion.3
  27.7 1.3 add_convert_fusion.11
  29.0 2.4 collective-permute-start.2
  31.4 7.1 %collective-permute-done.2 = bf16[128,1024]{1,0:T(8,128)(2,1)S(1)} collective-permute-done((bf16[128,1024]{1,0:T(8,128)(2,1)S(1)}, bf16[128,1024]{1,0:T(8,128)(2,1)S(1)}, u32[]{:S(2)}, u32[]{:S(2)}) %collective-permute-start.2) | collective-permute-done | bytes 262176 | tf_op jit(solution)/shard_map/ppermute | solution.py:15
  38.5 7.5 %conditional.5 = (f32[64,1024]{1,0:T(8,128)S(1)}, f32[192,1024]{1,0:T(8,128)}, f32[128,1024]{1,0:T(8,128)S(1)}, f32[3072,1024]{1,0:T(8,128)}) conditional(s32[]{:T(128)} %convert_element_type.146, () %tuple.42, (pred[]{:T(512)}, s32[1,128]{1,0:T(1,128)}, s32[1,128]{1,0:T(1,128)}, pred[128]{0:T(512)(128)(4,1)S(1)}, bf16[128,3072]{1,0:T(8,128)(2,1)S(1)}, ...), branch_computations={%region_4.5_spmd, %region_5.6_spmd} | conditional | flops 2457610496 | bytes 90375664 | solution.py:117
  38.5 6.2 %broadcast.213.clone = f32[3072,1024]{1,0:T(8,128)} broadcast(f32[]{:T(128)} %constant.132.clone), dimensions={} | broadcast | bytes 12582916 | tf_op jit(solution)/shard_map/broadcast.37
  46.9 1.3 collective-permute-start.3
  48.2 2.8 collective-permute-done.3
  51.0 1.3 multiply_reduce_fusion.2
  52.2 1.3 add_convert_fusion.10
  53.5 2.4 collective-permute-start.4
  55.9 62.1 %collective-permute-done.4 = bf16[128,1024]{1,0:T(8,128)(2,1)S(1)} collective-permute-done((bf16[128,1024]{1,0:T(8,128)(2,1)S(1)}, bf16[128,1024]{1,0:T(8,128)(2,1)S(1)}, u32[]{:S(2)}, u32[]{:S(2)}) %collective-permute-start.4) | collective-permute-done | bytes 262176 | tf_op jit(solution)/shard_map/ppermute | solution.py:15
  118.0 36.4 %conditional.6 = (f32[64,1024]{1,0:T(8,128)S(1)}, f32[192,1024]{1,0:T(8,128)}, f32[128,1024]{1,0:T(8,128)S(1)}, f32[3072,1024]{1,0:T(8,128)}) conditional(s32[]{:T(128)} %convert_element_type.149, () %tuple.44, (pred[]{:T(512)}, s32[1,128]{1,0:T(1,128)}, s32[1,128]{1,0:T(1,128)}, pred[128]{0:T(512)(128)(4,1)S(1)}, bf16[128,3072]{1,0:T(8,128)(2,1)S(1)}, ...), branch_computations={%region_7.8_spmd, %region_8.9_spmd} | conditional | flops 2457610496 | bytes 90375664 | solution.py:117
  118.4 3.9 fusion.185
  122.9 1.5 fusion.94
  124.4 2.2 fusion.186
  128.6 2.7 dynamic_update_slice.31
  131.2 1.1 slice_add_fusion.4
  132.4 2.8 dynamic_update_slice.32
  135.2 6.4 %convolution_bitcast_fusion.4 = f32[3072,1024]{0,1:T(8,128)} fusion(bf16[128,1024]{1,0:T(8,128)(2,1)S(1)} %get-tuple-element.190, bf16[128,3072]{1,0:T(8,128)(2,1)S(1)} %get-tuple-element.122), kind=kOutput, calls=%fused_computation.162 | convolution fusion | flops 805306368 | bytes 13631488 | tf_op jit(solution)/shard_map/cond/branch_1_fun/dot_general | solution.py:84
  141.6 12.6 %copy.24 = f32[3072,1024]{1,0:T(8,128)} copy(f32[3072,1024]{0,1:T(8,128)} %convolution_bitcast_fusion.4) | data formatting | bytes 25165824 | tf_op jit(solution)/shard_map/cond | solution.py:117
  154.4 1.0 slice.222
  155.4 1.3 collective-permute-start.5
  156.7 3.3 collective-permute-done.5
  160.0 1.3 multiply_reduce_fusion.1
  161.3 1.3 add_convert_fusion.9
  162.6 1.9 collective-permute-start.6
  164.5 7.2 %collective-permute-done.6 = bf16[128,1024]{1,0:T(8,128)(2,1)S(1)} collective-permute-done((bf16[128,1024]{1,0:T(8,128)(2,1)S(1)}, bf16[128,1024]{1,0:T(8,128)(2,1)S(1)}, u32[]{:S(2)}, u32[]{:S(2)}) %collective-permute-start.6) | collective-permute-done | bytes 262176 | tf_op jit(solution)/shard_map/ppermute | solution.py:15
  171.8 7.5 %conditional.7 = (f32[64,1024]{1,0:T(8,128)S(1)}, f32[192,1024]{1,0:T(8,128)}, f32[128,1024]{1,0:T(8,128)S(1)}, f32[3072,1024]{1,0:T(8,128)}) conditional(s32[]{:T(128)} %convert_element_type.152, () %tuple.46, (pred[]{:T(512)}, s32[1,128]{1,0:T(1,128)}, s32[1,128]{1,0:T(1,128)}, pred[128]{0:T(512)(128)(4,1)S(1)}, ...), branch_computations={%region_10.11_spmd, %region_11.12_spmd} | conditional | flops 2457610496 | bytes 90375664 | solution.py:117
  171.8 6.1 %broadcast.241.clone = f32[3072,1024]{1,0:T(8,128)} broadcast(f32[]{:T(128)} %constant.188.clone), dimensions={} | broadcast | bytes 12582916 | tf_op jit(solution)/shard_map/broadcast.81
  177.9 1.0 broadcast.243
  179.3 1.9 add_add_fusion.1
  181.2 23.2 %add_add_fusion = f32[3072,1024]{1,0:T(8,128)} fusion(f32[3072,1024]{1,0:T(8,128)} %get-tuple-element.179, f32[3072,1024]{1,0:T(8,128)} %get-tuple-element.178, f32[3072,1024]{1,0:T(8,128)} %get-tuple-element.176, f32[3072,1024]{1,0:T(8,128)} %get-tuple-element.177), kind=kLoop, calls=%fused_computation.324 | loop fusion | flops 9437184 | bytes 62914560 | tf_op jit(solution)/shard_map/add | solution.py:129
  204.5 1.0 slice.221
  205.5 1.3 collective-permute-start.7
  207.5 183.1 %all-reduce.11.cloned.1.call-done = f32[64,1024]{1,0:T(8,128)} async-done(((f32[64,1024]{1,0:T(8,128)}), f32[64,1024]{1,0:T(8,128)}) %all-reduce.11.cloned.1.call-update) | async-done | bytes 262160
  390.6 2.0 dynamic-slice_bitcast_fusion
  392.6 1.3 multiply_reduce_fusion
  393.8 2.0 fusion.179
  395.9 159.7 %reduce-scatter.2.cloned.1.call-done = f32[48,1024]{1,0:T(8,128)} async-done(((f32[3072,1024]{1,0:T(8,128)}), f32[48,1024]{1,0:T(8,128)}) %reduce-scatter.2.cloned.1.call-update) | async-done | bytes 196624 | tf_op jit(solution)/shard_map/reduce_scatter | solution.py:134
  (78 shorter events, 8.7 us)
Async XLA Ops:
  7.2 383.4 %all-reduce.11.cloned.1.call-start = ((), (), s32[]{:S(2)}) async-start(), calls=%async_computation.2 | async-start | bytes 524288
  9.4 4.2 collective-permute-start
  12.1 1.9 copy-start.18
  14.0 12.4 %copy-start = (bf16[1,1,128,1024]{3,2,1,0:T(8,128)(2,1)S(1)}, bf16[1,1,128,1024]{3,2,1,0:T(8,128)(2,1)}, u32[]{:S(2)}) copy-start(bf16[1,1,128,1024]{3,2,1,0:T(8,128)(2,1)} %param.16) | copy-start | bytes 786436
  21.3 17.2 %copy-start.9 = (f32[64,1024]{1,0:T(8,128)}, f32[64,1024]{1,0:T(8,128)S(1)}, u32[]{:S(2)}) copy-start(f32[64,1024]{1,0:T(8,128)S(1)} %get-tuple-element.170) | copy-start | bytes 786436
  22.1 4.3 collective-permute-start.1
  29.0 9.5 %copy-start.12 = (bf16[128,1024]{1,0:T(8,128)(2,1)}, bf16[128,1024]{1,0:T(8,128)(2,1)S(1)}, u32[]{:S(2)}) copy-start(bf16[128,1024]{1,0:T(8,128)(2,1)S(1)} %add_convert_fusion.11) | copy-start | bytes 786436
  29.0 9.4 %collective-permute-start.2 = (bf16[128,1024]{1,0:T(8,128)(2,1)S(1)}, bf16[128,1024]{1,0:T(8,128)(2,1)S(1)}, u32[]{:S(2)}, u32[]{:S(2)}) collective-permute-start(bf16[128,1024]{1,0:T(8,128)(2,1)S(1)} %add_convert_fusion.11), channel_id=1, source_target_pairs={{8,0},{16,8},{24,16},{9,1},{17,9},{25,17},{10,2},{18,10},{26,18},{... | collective-permute-start | bytes 786440 | tf_op jit(solution)/shard_map/ppermute | solution.py:15
  46.0 72.0 %copy-start.10 = (f32[64,1024]{1,0:T(8,128)}, f32[64,1024]{1,0:T(8,128)S(1)}, u32[]{:S(2)}) copy-start(f32[64,1024]{1,0:T(8,128)S(1)} %get-tuple-element.171) | copy-start | bytes 786436
  46.9 4.1 collective-permute-start.3
  53.5 64.5 %copy-start.14 = (bf16[128,1024]{1,0:T(8,128)(2,1)}, bf16[128,1024]{1,0:T(8,128)(2,1)S(1)}, u32[]{:S(2)}) copy-start(bf16[128,1024]{1,0:T(8,128)(2,1)S(1)} %add_convert_fusion.10) | copy-start | bytes 786436
  53.5 64.4 %collective-permute-start.4 = (bf16[128,1024]{1,0:T(8,128)(2,1)S(1)}, bf16[128,1024]{1,0:T(8,128)(2,1)S(1)}, u32[]{:S(2)}, u32[]{:S(2)}) collective-permute-start(bf16[128,1024]{1,0:T(8,128)(2,1)S(1)} %add_convert_fusion.10), channel_id=1, source_target_pairs={{8,0},{16,8},{24,16},{9,1},{17,9},{25,17},{10,2},{18,10},{26,18},{... | collective-permute-start | bytes 786440 | tf_op jit(solution)/shard_map/ppermute | solution.py:15
  118.3 6.1 %slice-start.4 = ((s8[6291456]{0:T(1024)(128)(4,1)}), s8[4194304]{0:T(1024)(128)(4,1)S(1)}, s32[]{:S(2)}) async-start(s8[6291456]{0:T(1024)(128)(4,1)} %bitcast.618), calls=%async_computation.7 | async-start | bytes 8388608 | tf_op jit(solution)/shard_map/cond
  118.3 4.0 copy-start.3
  118.3 4.2 copy-start.20
  118.3 4.2 copy-start.32
  118.3 4.5 copy-start.24
  118.3 4.5 copy-start.28
  118.4 6.0 %slice-start.5 = ((s8[6291456]{0:T(1024)(128)(4,1)}), s8[2097152]{0:T(1024)(128)(4,1)S(1)}, s32[]{:S(2)}) async-start(s8[6291456]{0:T(1024)(128)(4,1)} %bitcast.618), calls=%async_computation.8 | async-start | bytes 4194304 | tf_op jit(solution)/shard_map/cond
  141.5 12.9 %copy-start.7 = (f32[128,1024]{1,0:T(8,128)S(1)}, f32[128,1024]{1,0:T(8,128)}, u32[]{:S(2)}) copy-start(f32[128,1024]{1,0:T(8,128)} %get-tuple-element.220) | copy-start | bytes 1572868 | tf_op jit(solution)/shard_map/cond
  154.4 17.3 %copy-start.11 = (f32[64,1024]{1,0:T(8,128)}, f32[64,1024]{1,0:T(8,128)S(1)}, u32[]{:S(2)}) copy-start(f32[64,1024]{1,0:T(8,128)S(1)} %get-tuple-element.172) | copy-start | bytes 786436
  155.4 4.6 collective-permute-start.5
  162.6 9.2 %copy-start.16 = (bf16[128,1024]{1,0:T(8,128)(2,1)}, bf16[128,1024]{1,0:T(8,128)(2,1)S(1)}, u32[]{:S(2)}) copy-start(bf16[128,1024]{1,0:T(8,128)(2,1)S(1)} %add_convert_fusion.9) | copy-start | bytes 786436
  162.6 9.1 %collective-permute-start.6 = (bf16[128,1024]{1,0:T(8,128)(2,1)S(1)}, bf16[128,1024]{1,0:T(8,128)(2,1)S(1)}, u32[]{:S(2)}, u32[]{:S(2)}) collective-permute-start(bf16[128,1024]{1,0:T(8,128)(2,1)S(1)} %add_convert_fusion.9), channel_id=1, source_target_pairs={{8,0},{16,8},{24,16},{9,1},{17,9},{25,17},{10,2},{18,10},{26,18},{... | collective-permute-start | bytes 786440 | tf_op jit(solution)/shard_map/ppermute | solution.py:15
  181.2 374.4 %reduce-scatter.2.cloned.1.call-start = ((), (), s32[]{:S(2)}) async-start(), calls=%async_computation.1 | async-start | bytes 12779520 | tf_op jit(solution)/shard_map/reduce_scatter | solution.py:134
  204.5 2.4 copy-start.34
  204.5 189.4 %copy-start.13 = (bf16[128,1024]{1,0:T(8,128)(2,1)S(1)}, bf16[128,1024]{1,0:T(8,128)(2,1)}, u32[]{:S(2)}) copy-start(bf16[128,1024]{1,0:T(8,128)(2,1)} %copy-done.12) | copy-start | bytes 786436
  204.5 189.4 %copy-start.15 = (bf16[128,1024]{1,0:T(8,128)(2,1)S(1)}, bf16[128,1024]{1,0:T(8,128)(2,1)}, u32[]{:S(2)}) copy-start(bf16[128,1024]{1,0:T(8,128)(2,1)} %copy-done.14) | copy-start | bytes 786436
  204.5 189.4 %copy-start.17 = (bf16[128,1024]{1,0:T(8,128)(2,1)S(1)}, bf16[128,1024]{1,0:T(8,128)(2,1)}, u32[]{:S(2)}) copy-start(bf16[128,1024]{1,0:T(8,128)(2,1)} %copy-done.16) | copy-start | bytes 786436
  205.5 187.0 %collective-permute-start.7 = (bf16[64,1024]{1,0:T(8,128)(2,1)S(1)}, bf16[64,1024]{1,0:T(8,128)(2,1)S(1)}, u32[]{:S(2)}, u32[]{:S(2)}) collective-permute-start(bf16[64,1024]{1,0:T(8,128)(2,1)S(1)} %slice.221), channel_id=1, source_target_pairs={{1,0},{2,1},{3,2},{4,3},{5,4},{6,5},{7,6},{9,8},{10,9},{11,10},{12... | collective-permute-start | bytes 393224 | tf_op jit(solution)/shard_map/ppermute | solution.py:15
Sparse Core Ops, SparseCore 0:
  181.3 209.2 all-reduce.10
  395.4 160.0 reduce-scatter.1
where the time goes:
time: 564 us; the launch traced here: 562 us
  waiting for transfers between devices  428 us (76%)
  local copies, waits for them, and re-layouts  47.3 us (8%)
  other arithmetic  42.5 us (8%)
  between operations  15.1 us (3%)
  matrix products  14.8 us (3%)
  starting transfers between devices  13.6 us (2%)
    unnamed x3, waiting for transfers between devices  183 us
    reduce_scatter x1, waiting for transfers between devices, on_device(): lax.psum_scatter(conv_total, ('dp', 'seq'), scatter_dimension=0, tiled=True)  160 us
    ppermute x8, waiting for transfers between devices, from_behind(): return lax.ppermute(array, axis, pairs)  85.4 us
    add x1, other arithmetic, on_device(): conv_total = conv_total + conv_part  23.2 us
    another operation x12, local copies, waits for them, and re-layouts  21.7 us
    ppermute x8, starting transfers between devices, from_behind(): return lax.ppermute(array, axis, pairs)  13.5 us
    cond x1, local copies, waits for them, and re-layouts, on_device(): lax.cond(active, active_work, spare_work, incoming)  12.6 us
  transfers between devices with their start and end apart: 10, of which 8 were waited for; matrix products, arithmetic and copies ran while one was open for 6% of the time, Pallas kernels for 0%

commit v1 on v0

v1 whole, which is shorter than its diff:
```python
import functools

import jax
import jax.numpy as jnp
from jax import lax
from jax.experimental import pallas as pl
from jax.experimental.pallas import tpu as pltpu
from jax.sharding import PartitionSpec as P

EPS = 1e-06
GELU_C = 0.7978845608028654
GELU_A = 0.044715
BF = jnp.bfloat16
F32 = jnp.float32
ROWS = 128
HALO = 64
EXT = ROWS + HALO
WIDTH = 1024
KERNEL = 3
KINDS = 64
GROUP = 8
OWN = KERNEL * WIDTH // (GROUP * GROUP)
CONV_ROWS = GROUP * OWN
SEND_ROWS = CONV_ROWS + 16
NT = (((1,), (1,)), ((), ()))


def spacing():
    return jnp.right_shift(jnp.int32(ROWS // 4), lax.axis_index("pipe"))


def rms_inv(x):
    return lax.rsqrt(jnp.mean(x * x, axis=-1, keepdims=True) + EPS)


def gelu_grad(x):
    x2 = x * x
    th = jnp.tanh(GELU_C * x * (1.0 + GELU_A * x2))
    slope = GELU_C * (1.0 + 3.0 * GELU_A * x2)
    value = 0.5 * x * (1.0 + th)
    grad = 0.5 * (1.0 + th) + 0.5 * x * (1.0 - th * th) * slope
    return value, grad


def shifted(base, sign, copy):
    d = spacing()
    is_last = lax.axis_index("pipe") == lax.axis_size("pipe") - 1
    least = ROWS // 4 >> (lax.axis_size("pipe") - 1)

    @pl.when(is_last)
    def _():
        for tap in range(KERNEL):
            copy(tap, base + sign * tap * least)

    @pl.when(jnp.logical_not(is_last))
    def _():
        for tap in range(KERNEL):
            copy(tap, pl.multiple_of(base + sign * tap * d, 8))


def input_side(g_ref, tap_ref, grad_out, x, w_ref):
    def copy(tap, start):
        tap_ref[tap, :ROWS] = g_ref[pl.ds(start, ROWS), :].astype(BF)

    shifted(0, 1, copy)
    grad_normed = None
    for tap in range(KERNEL):
        part = lax.dot_general(
            tap_ref[tap, :ROWS],
            w_ref[tap * WIDTH : (tap + 1) * WIDTH, :],
            NT,
            preferred_element_type=F32,
        )
        grad_normed = part if grad_normed is None else grad_normed + part
    inv = rms_inv(x)
    normed = x * inv
    inner = jnp.mean(grad_normed * normed, axis=-1, keepdims=True)
    return (grad_out + inv * (grad_normed - normed * inner)).astype(BF)


def first_kernel(
    len_ref, x_ref, prev_ref, own_ref, next_ref, w_ref, table_ref, head_ref,
    gp_ref, top_ref, gin_ref, edge_ref, normed_ref, g_ref, tap_ref,
):
    shard = lax.axis_index("seq")
    x_ext = jnp.concatenate(
        [prev_ref[...], x_ref[...], next_ref[:HALO, :]], axis=0
    ).astype(F32)
    normed_ref[...] = x_ext * rms_inv(x_ext)
    eye = (
        lax.broadcasted_iota(jnp.int32, (ROWS, ROWS), 0)
        == lax.broadcasted_iota(jnp.int32, (ROWS, ROWS), 1)
    ).astype(F32).astype(BF)
    meta = jnp.concatenate(
        [
            lax.dot_general(eye, ref[HALO:, :ROWS], NT, preferred_element_type=F32)
            for ref in (own_ref, next_ref)
        ],
        axis=0,
    )[:EXT]
    ids = meta[:, 0:1].astype(jnp.int32)
    label_y = meta[:, 1:2]
    label_z = label_y * meta[:, 2:3]
    onehot = (
        lax.broadcasted_iota(jnp.int32, (EXT, KINDS), 1) == ids
    ).astype(F32).astype(BF)
    def copy(tap, start):
        tap_ref[tap] = normed_ref[pl.ds(start, EXT), :].astype(BF)

    shifted(HALO, -1, copy)
    pre = jnp.dot(onehot, table_ref[...], preferred_element_type=F32)
    for tap in range(KERNEL):
        pre = pre + jnp.dot(
            tap_ref[tap],
            w_ref[tap * WIDTH : (tap + 1) * WIDTH, :],
            preferred_element_type=F32,
        )
    value, grad = gelu_grad(pre)
    gp_ref[...] = grad
    out = (x_ext[HALO:] + value).astype(BF).astype(F32)
    head = head_ref[...].astype(F32)
    first = jnp.sum(out * head[0:1], axis=-1, keepdims=True)
    second = jnp.sum(out * head[1:2], axis=-1, keepdims=True)
    a_pos, a_neg = jax.nn.sigmoid(first), jax.nn.sigmoid(-first)
    b_pos, b_neg = jax.nn.sigmoid(second), jax.nn.sigmoid(-second)
    rest = (1.0 - label_z) / (a_neg + a_pos * b_neg)
    grad_first = (
        (1.0 - label_y) * a_pos
        - (label_y + label_z) * a_neg
        + rest * (a_pos * a_neg * b_pos)
    )
    grad_second = rest * (a_pos * b_pos * b_neg) - label_z * b_neg
    position = shard * ROWS + lax.broadcasted_iota(jnp.int32, (EXT, 1), 0)
    valid = position < len_ref[0]
    grad_first = jnp.where(valid, grad_first, 0.0)
    grad_second = jnp.where(valid, grad_second, 0.0)
    top = grad_first * head[0:1] + grad_second * head[1:2]
    top_ref[...] = top

    g_ref[...] = top * grad
    gin = input_side(g_ref, tap_ref, top[:ROWS], x_ext[HALO : HALO + ROWS], w_ref)
    gin_ref[...] = gin
    edge_ref[...] = gin[: edge_ref.shape[0]]


def merged(main_ref, halo_ref, top_ref):
    is_last = lax.axis_index("pipe") == lax.axis_size("pipe") - 1
    halo = halo_ref[...].astype(F32)
    if halo.shape[0] < HALO:
        halo = jnp.concatenate([halo, jnp.zeros((HALO - halo.shape[0], WIDTH), F32)], axis=0)
    incoming = jnp.concatenate([main_ref[...].astype(F32), halo], axis=0)
    return jnp.where(is_last, top_ref[...], incoming)


def tick_kernel(main_ref, halo_ref, top_ref, gp_ref, x_ref, w_ref, gin_ref, edge_ref, g_ref, tap_ref):
    grad_out = merged(main_ref, halo_ref, top_ref)
    g_ref[...] = grad_out * gp_ref[...]
    gin = input_side(g_ref, tap_ref, grad_out[:ROWS], x_ref[...].astype(F32), w_ref)
    gin_ref[...] = gin
    edge_ref[...] = gin[: edge_ref.shape[0]]


def pack_kernel(main_ref, halo_ref, top_ref, gp_ref, ids_ref, g_ref):
    g = (merged(main_ref, halo_ref, top_ref) * gp_ref[...]).astype(BF)
    ids = ids_ref[...].astype(F32).astype(BF)
    for block in range(GROUP):
        g_ref[block, :EXT] = g[:, block * ROWS : (block + 1) * ROWS]
        g_ref[block, EXT:] = jnp.broadcast_to(ids, (16, ROWS))


def last_kernel(main_ref, halo_ref, top_ref, gp_ref, x_ref, w_ref, gin_ref, g_ref, tap_ref):
    grad_out = merged(main_ref, halo_ref, top_ref)
    g_ref[...] = grad_out * gp_ref[...]
    gin_ref[...] = input_side(g_ref, tap_ref, grad_out[:ROWS], x_ref[...].astype(F32), w_ref)


def normed_kernel(*refs):
    out_ref = refs[-1]
    for place, ref in enumerate(refs[:-1]):
        x = ref[...].astype(F32)
        out_ref[:, place * ROWS : (place + 1) * ROWS] = (x * rms_inv(x)).T.astype(BF)


def weight_kernel(offsets, g_ref, nt_ref, out_ref, wide_ref, rhs_ref, hot_ref):
    me = lax.axis_index("dp")
    wide_ref[...] = g_ref[...].astype(F32)
    line = lax.broadcasted_iota(jnp.int32, (ROWS, ROWS), 0)
    kind = jnp.where(line % 16 < GROUP, GROUP * (line % 16) + line // 16, -1).astype(F32)

    def copy(tap, start):
        for place, offset in enumerate(offsets):
            user = lax.rem(me + offset, GROUP)
            rhs_ref[place * ROWS : (place + 1) * ROWS, tap * ROWS : (tap + 1) * ROWS] = (
                wide_ref[user, pl.ds(start, ROWS), :].astype(BF)
            )

    shifted(0, 1, copy)
    for place, offset in enumerate(offsets):
        ids = wide_ref[lax.rem(me + offset, GROUP), EXT : EXT + 1, :]
        hot_ref[:, place * ROWS : (place + 1) * ROWS] = (kind == ids).astype(F32).astype(BF)
    conv = jnp.dot(nt_ref[...], rhs_ref[...], preferred_element_type=F32).astype(BF)
    kinds = jnp.dot(hot_ref[...], rhs_ref[:, :ROWS], preferred_element_type=F32).astype(BF)
    for group in range(GROUP):
        for shard in range(GROUP):
            row = (group * GROUP + shard) * OWN
            for piece in range(OWN // 16):
                tap, feature = divmod(row + piece * 16, WIDTH)
                out_ref[shard, group * OWN + piece * 16 : group * OWN + (piece + 1) * 16] = conv[
                    feature : feature + 16, tap * ROWS : (tap + 1) * ROWS
                ]
    for shard in range(GROUP):
        out_ref[shard, CONV_ROWS:] = kinds[shard * 16 : (shard + 1) * 16]


def sum_kernel(in_ref, out_ref):
    total = in_ref[0].astype(F32)
    for source in range(1, GROUP):
        total = total + in_ref[source].astype(F32)
    for group in range(GROUP):
        out_ref[group, :OWN] = total[group * OWN : (group + 1) * OWN].astype(BF)
        out_ref[group, OWN:] = jnp.broadcast_to(
            total[CONV_ROWS + group : CONV_ROWS + group + 1], (16, ROWS)
        ).astype(BF)


def place_kernel(in_ref, conv_ref, kind_ref):
    for block in range(GROUP):
        lanes = slice(block * ROWS, (block + 1) * ROWS)
        conv_ref[:, lanes] = in_ref[block, :OWN].astype(F32)
        kind_ref[:, lanes] = in_ref[block, OWN : OWN + 1].astype(F32)


def whole(space=pltpu.VMEM):
    return pl.BlockSpec(memory_space=space)


def call(kernel, outs, args, scratch=(), limit=24, first_smem=False, name=None):
    specs = [whole() for _ in args]
    if first_smem:
        specs[0] = whole(pltpu.SMEM)
    many = isinstance(outs, (list, tuple))
    return pl.pallas_call(
        kernel,
        out_shape=outs,
        in_specs=specs,
        out_specs=[whole() for _ in outs] if many else whole(),
        scratch_shapes=list(scratch),
        compiler_params=pltpu.CompilerParams(vmem_limit_bytes=limit << 20),
        name=name,
    )(*args)


def shaped(shape, dtype):
    return jax.ShapeDtypeStruct(shape, dtype)


def on_device(
    section_input, event_ids, lengths, clicks, conversions, conv_weight, type_table, head_weight
):
    x = section_input[0, 0]
    weight = conv_weight[0]
    table = type_table[0]
    shards = lax.axis_size("seq")
    sections = lax.axis_size("pipe")
    users = lax.axis_size("dp")

    meta = jnp.concatenate([event_ids, clicks, conversions], axis=0).astype(BF)
    own = jnp.concatenate([x[:HALO], jnp.pad(meta, ((0, 13), (0, WIDTH - ROWS)))], axis=0)
    following = lax.ppermute(own, "seq", [(i + 1, i) for i in range(shards - 1)])
    preceding = lax.ppermute(x[ROWS - HALO :], "seq", [(i, i + 1) for i in range(shards - 1)])

    def around(array, by):
        return lax.ppermute(array, "dp", [(i, (i + by) % users) for i in range(users)])

    def to_previous(array):
        return lax.ppermute(
            array, "pipe", [(i, i - 1) for i in range(1, sections)]
        )

    def to_previous_corner(array):
        pairs = [
            (p * shards + s, (p - 1) * shards + s - 1)
            for p in range(1, sections)
            for s in range(1, shards)
        ]
        return lax.ppermute(array, ("pipe", "seq"), pairs)

    wide = shaped((EXT, WIDTH), F32)
    narrow = shaped((ROWS, WIDTH), BF)
    scratch_g = pltpu.VMEM((EXT, WIDTH), F32)
    scratch_tap = pltpu.VMEM((KERNEL, EXT, WIDTH), BF)
    gp, top, gin, edge = call(
        first_kernel,
        [wide, wide, narrow, shaped((16, WIDTH), BF)],
        (lengths, x, preceding, own, following, weight, table, head_weight),
        [pltpu.VMEM((EXT + HALO, WIDTH), F32), scratch_g, scratch_tap],
        first_smem=True,
        name="first",
    )
    forward, backward = x, x
    blocks, offsets = [x], [0]
    for tick in range(1, sections):
        main = to_previous(gin)
        halo = to_previous_corner(edge)
        forward, backward = around(forward, 1), around(backward, -1)
        blocks += [forward, backward]
        offsets += [users - tick, tick]
        if tick + 1 < sections:
            gin, edge = call(
                tick_kernel,
                [narrow, shaped((16 << tick, WIDTH), BF)],
                (main, halo, top, gp, x, weight),
                [scratch_g, scratch_tap],
                name="tick",
            )
    blocks.append(around(forward, 1))
    offsets.append(users // 2)
    normed_t = call(
        normed_kernel, shaped((WIDTH, users * ROWS), BF), tuple(blocks), name="normed"
    )
    packed = call(
        pack_kernel, shaped((GROUP, EXT + 16, ROWS), BF), (main, halo, top, gp, event_ids), name="pack"
    )
    spread = lax.all_to_all(packed, "dp", 0, 0, tiled=True)
    gin = call(
        last_kernel, narrow, (main, halo, top, gp, x, weight), [scratch_g, scratch_tap], name="last"
    )
    partial = call(
        functools.partial(weight_kernel, tuple(offsets)),
        shaped((GROUP, SEND_ROWS, ROWS), BF),
        (spread, normed_t),
        [
            pltpu.VMEM((GROUP, EXT + 16, ROWS), F32),
            pltpu.VMEM((GROUP * ROWS, KERNEL * ROWS), BF),
            pltpu.VMEM((ROWS, GROUP * ROWS), BF),
        ],
        name="weight",
    )
    gathered = lax.all_to_all(partial, "seq", 0, 0, tiled=True)
    summed = call(sum_kernel, shaped((GROUP, HALO, ROWS), BF), (gathered,), name="sum")
    final = lax.all_to_all(summed, "dp", 0, 0, tiled=True)
    conv_share, type_share = call(
        place_kernel,
        [shaped((OWN, WIDTH), F32), shaped((1, WIDTH), F32)],
        (final,),
        name="place",
    )
    return (conv_share[None], type_share[None], gin[None, None])


def solution(mesh):
    placed = (
        P("pipe", "dp", "seq", None),
        P("dp", "seq"),
        P("dp"),
        P("dp", "seq"),
        P("dp", "seq"),
        P("pipe", None, None),
        P("pipe", None, None),
        P(),
    )
    return jax.shard_map(
        on_device,
        mesh=mesh,
        in_specs=placed,
        out_specs=(
            P("pipe", ("dp", "seq"), None),
            P("pipe", ("dp", "seq"), None),
            P("pipe", "dp", "seq", None),
        ),
        check_vma=False,
    )
```

time: 564 us -> 137 us (0.24)
  waiting for transfers between devices: 428 us -> 36.3 us
  other arithmetic: 42.5 us -> 2 us
  local copies, waits for them, and re-layouts: 47.3 us -> 11.1 us
  starting transfers between devices: 13.6 us -> 45.2 us
  Pallas kernels: 0 us -> 23.4 us
  blocking collectives: 0 us -> 16.1 us
  matrix products: 14.8 us -> 0 us
  between operations: 15.1 us -> 1.43 us
    unnamed x3 -> x0, waiting for transfers between devices: 183 us -> none
    reduce_scatter x1 -> x0, waiting for transfers between devices: 160 us -> none  [on_device(): lax.psum_scatter(conv_total, ('dp', 'seq'), scatter_dimension=0, tiled=True)]
    ppermute x8 -> x15, waiting for transfers between devices: 85.4 us -> 34.1 us  [the longest x7 19.1 us: around(): lax.ppermute(array, 'dp', [(i, (i + by) % users) for i in range(users)])]
    add x4 -> x0, other arithmetic: 27.1 us -> none  [the longest x1 23.2 us: on_device(): conv_total = conv_total + conv_part]
    pallas_call x0 -> x9, Pallas kernels: none -> 23.4 us  [call(): pl.pallas_call(kernel, out_shape=outs, in_specs=specs, out_specs=[whole()...]
    another operation x12 -> x0, local copies, waits for them, and re-layouts: 21.7 us -> none
    ppermute x8 -> x15, starting transfers between devices: 13.5 us -> 30.1 us  [the longest x3 12.2 us: to_previous(): return lax.ppermute(array, 'pipe', [(i, i - 1) for i in range(1, sections)])]
    all_to_all x0 -> x1, blocking collectives: none -> 16.1 us  [on_device(): gathered = lax.all_to_all(partial, 'seq', 0, 0, tiled=True)]
  transfers between devices with their start and end apart: 10 -> 17, of which waited for: 8 -> 9; matrix products, arithmetic and copies ran while one was open for 6% -> 0% of each run, Pallas kernels for 0% -> 8%
where the time goes in v1:
time: 137 us; the launch traced here: 136 us
  starting transfers between devices  45.2 us (33%)
  waiting for transfers between devices  36.3 us (26%)
  Pallas kernels  23.4 us (17%)
  blocking collectives  16.1 us (12%)
  local copies, waits for them, and re-layouts  11.1 us (8%)
  other arithmetic  2 us (1%)
  between operations  1.43 us (1%)
    pallas_call x9, Pallas kernels, call(): pl.pallas_call(kernel, out_shape=outs, in_specs=specs, out_specs=[whole()...  23.4 us
    ppermute x7, waiting for transfers between devices, around(): lax.ppermute(array, 'dp', [(i, (i + by) % users) for i in range(users)])  19.1 us
    all_to_all x1, blocking collectives, on_device(): gathered = lax.all_to_all(partial, 'seq', 0, 0, tiled=True)  16.1 us
    ppermute x3, waiting for transfers between devices, to_previous_corner(): return lax.ppermute(array, ('pipe', 'seq'), pairs)  14.4 us
    ppermute x3, starting transfers between devices, to_previous(): return lax.ppermute(array, 'pipe', [(i, i - 1) for i in range(1, sections)])  12.2 us
    unnamed x16, local copies, waits for them, and re-layouts  10.1 us
    ppermute x7, starting transfers between devices, around(): lax.ppermute(array, 'dp', [(i, (i + by) % users) for i in range(users)])  9.73 us
    all_to_all x1, starting transfers between devices, on_device(): spread = lax.all_to_all(packed, 'dp', 0, 0, tiled=True)  8.15 us
  transfers between devices with their start and end apart: 17, of which 9 were waited for; matrix products, arithmetic and copies ran while one was open for 0% of the time, Pallas kernels for 8%

profile of v1, /device:TPU:8, one launch (start us, length us, event | category | flops | bytes accessed | tf_op | source)
XLA Modules:
  0.0 135.6 jit_solution(14525082456174217174)
XLA Ops:
  0.6 1.0 slice_bitcast_fusion
  1.6 0.7 convert.10
  2.3 0.7 convert.11
  2.9 0.7 convert.9
  3.6 1.3 collective-permute-start.1
  4.9 3.0 %collective-permute-start = (bf16[64,1024]{1,0:T(8,128)(2,1)S(1)}, bf16[64,1024]{1,0:T(8,128)(2,1)S(1)}, u32[]{:S(2)}, u32[]{:S(2)}) collective-permute-start(bf16[64,1024]{1,0:T(8,128)(2,1)S(1)} %get-tuple-element.24), channel_id=1, source_target_pairs={{0,1},{1,2},{2,3},{3,4},{4,5},{5,6},{6,7},{8,9},{9,10},{10,11},{11... | collective-permute-start | bytes 393224 | tf_op jit(solution)/shard_map/ppermute | solution.py:270
  8.6 0.3 collective-permute-done.prev_ref
  8.9 2.8 %copy-done = bf16[1,3072,1024]{2,1,0:T(8,128)(2,1)S(1)} copy-done((bf16[1,3072,1024]{2,1,0:T(8,128)(2,1)S(1)}, bf16[1,3072,1024]{2,1,0:T(8,128)(2,1)}, u32[]{:S(2)}) %copy-start) | copy-done | bytes 6291480
  11.7 0.9 copy-done.5
  12.6 0.7 copy-done.6
  13.3 6.2 %first.1 = (f32[192,1024]{1,0:T(8,128)S(1)}, f32[192,1024]{1,0:T(8,128)S(1)}, bf16[128,1024]{1,0:T(8,128)(2,1)S(1)}, bf16[16,1024]{1,0:T(8,128)(2,1)S(1)}) custom-call(s32[1]{0:T(128)S(6)} %copy.11.len_ref, bf16[128,1024]{1,0:T(8,128)(2,1)} %bitcast.x_ref.refs_0_, bf16[64,1024]{1,0:T(8,128)(2,1)S(1)} %collective-permute-done.prev_ref, ...), custom_call_target="tpu_custom_call" | custom-call | tf_op jit(solution)/shard_map/first/pallas_call | solution.py:242
  19.6 4.1 %collective-permute-start.2 = (bf16[128,1024]{1,0:T(8,128)(2,1)S(1)}, bf16[128,1024]{1,0:T(8,128)(2,1)S(1)}, u32[]{:S(2)}, u32[]{:S(2)}) collective-permute-start(bf16[128,1024]{1,0:T(8,128)(2,1)S(1)} %get-tuple-element.13), channel_id=1, source_target_pairs={{8,0},{16,8},{24,16},{9,1},{17,9},{25,17},{10,2},{18,10},{26,18},{... | collective-permute-start | bytes 786440 | tf_op jit(solution)/shard_map/ppermute | solution.py:276
  23.6 1.3 collective-permute-start.3
  24.9 6.4 %collective-permute-done.3.halo_ref = bf16[16,1024]{1,0:T(8,128)(2,1)S(1)} collective-permute-done((bf16[16,1024]{1,0:T(8,128)(2,1)S(1)}, bf16[16,1024]{1,0:T(8,128)(2,1)S(1)}, u32[]{:S(2)}, u32[]{:S(2)}) %collective-permute-start.3) | collective-permute-done | bytes 32800 | tf_op jit(solution)/shard_map/ppermute | solution.py:286
  31.3 0.0 collective-permute-done.2.main_ref
  31.3 3.5 %tick.2 = (bf16[128,1024]{1,0:T(8,128)(2,1)S(1)}, bf16[32,1024]{1,0:T(8,128)(2,1)S(1)}) custom-call(bf16[128,1024]{1,0:T(8,128)(2,1)S(1)} %collective-permute-done.2.main_ref, bf16[16,1024]{1,0:T(8,128)(2,1)S(1)} %collective-permute-done.3.halo_ref, f32[192,1024]{1,0:T(8,128)S(1)} %get-tuple-element.15.top_ref, f32[192,1024]{1,0:T(8,128)S(1)} %get-tuple-element.16.gp_ref, ...), custom_call_target="tpu_custom_call" | custom-call | tf_op jit(solution)/shard_map/tick/pallas_call | solution.py:242
  34.8 0.0 copy-start.7
  34.9 4.1 %collective-permute-start.4 = (bf16[128,1024]{1,0:T(8,128)(2,1)S(1)}, bf16[128,1024]{1,0:T(8,128)(2,1)S(1)}, u32[]{:S(2)}, u32[]{:S(2)}) collective-permute-start(bf16[128,1024]{1,0:T(8,128)(2,1)S(1)} %get-tuple-element.17), channel_id=1, source_target_pairs={{8,0},{16,8},{24,16},{9,1},{17,9},{25,17},{10,2},{18,10},{26,18},{... | collective-permute-start | bytes 786440 | tf_op jit(solution)/shard_map/ppermute | solution.py:276
  38.9 1.3 collective-permute-start.5
  40.2 0.3 collective-permute-start.8
  40.5 5.4 %collective-permute-done.5.halo_ref = bf16[32,1024]{1,0:T(8,128)(2,1)S(1)} collective-permute-done((bf16[32,1024]{1,0:T(8,128)(2,1)S(1)}, bf16[32,1024]{1,0:T(8,128)(2,1)S(1)}, u32[]{:S(2)}, u32[]{:S(2)}) %collective-permute-start.5) | collective-permute-done | bytes 65568 | tf_op jit(solution)/shard_map/ppermute | solution.py:286
  45.9 0.2 collective-permute-done.4.main_ref
  46.2 3.5 %tick.3 = (bf16[128,1024]{1,0:T(8,128)(2,1)S(1)}, bf16[64,1024]{1,0:T(8,128)(2,1)S(1)}) custom-call(bf16[128,1024]{1,0:T(8,128)(2,1)S(1)} %collective-permute-done.4.main_ref, bf16[32,1024]{1,0:T(8,128)(2,1)S(1)} %collective-permute-done.5.halo_ref, f32[192,1024]{1,0:T(8,128)S(1)} %get-tuple-element.15.top_ref, f32[192,1024]{1,0:T(8,128)S(1)} %get-tuple-element.16.gp_ref, ...), custom_call_target="tpu_custom_call" | custom-call | tf_op jit(solution)/shard_map/tick/pallas_call | solution.py:242
  49.7 4.0 %collective-permute-start.6 = (bf16[128,1024]{1,0:T(8,128)(2,1)S(1)}, bf16[128,1024]{1,0:T(8,128)(2,1)S(1)}, u32[]{:S(2)}, u32[]{:S(2)}) collective-permute-start(bf16[128,1024]{1,0:T(8,128)(2,1)S(1)} %get-tuple-element.19), channel_id=1, source_target_pairs={{8,0},{16,8},{24,16},{9,1},{17,9},{25,17},{10,2},{18,10},{26,18},{... | collective-permute-start | bytes 786440 | tf_op jit(solution)/shard_map/ppermute | solution.py:276
  53.7 1.3 collective-permute-start.7
  55.0 4.2 %collective-permute-start.9 = (bf16[128,1024]{1,0:T(8,128)(2,1)}, bf16[128,1024]{1,0:T(8,128)(2,1)S(1)}, u32[]{:S(2)}, u32[]{:S(2)}) collective-permute-start(bf16[128,1024]{1,0:T(8,128)(2,1)} %bitcast.x_ref.refs_0_), channel_id=1, source_target_pairs={{0,224},{32,0},{64,32},{96,64},{128,96},{160,128},{192,160},{224,1... | collective-permute-start | bytes 786440 | tf_op jit(solution)/shard_map/ppermute | solution.py:273
  59.2 0.0 collective-permute-start.10
  59.2 2.6 %collective-permute-done.7.halo_ref = bf16[64,1024]{1,0:T(8,128)(2,1)S(1)} collective-permute-done((bf16[64,1024]{1,0:T(8,128)(2,1)S(1)}, bf16[64,1024]{1,0:T(8,128)(2,1)S(1)}, u32[]{:S(2)}, u32[]{:S(2)}) %collective-permute-start.7) | collective-permute-done | bytes 131104 | tf_op jit(solution)/shard_map/ppermute | solution.py:286
  61.8 0.9 pack.1
  62.7 8.1 %all-to-all-start = ((bf16[8,208,128]{2,1,0:T(8,128)(2,1)}), bf16[8,208,128]{2,1,0:T(8,128)(2,1)S(1)}, u32[]{:S(2)}, u32[]{:S(2)}) async-start(bf16[8,208,128]{2,1,0:T(8,128)(2,1)} %pack.1), calls=%async_computation | async-start | bytes 851968 | tf_op jit(solution)/shard_map/all_to_all | solution.py:324
  70.9 3.2 %collective-permute-start.11 = (bf16[128,1024]{1,0:T(8,128)(2,1)S(1)}, bf16[128,1024]{1,0:T(8,128)(2,1)S(1)}, u32[]{:S(2)}, u32[]{:S(2)}) collective-permute-start(bf16[128,1024]{1,0:T(8,128)(2,1)S(1)} %collective-permute-done.9.refs_2_), channel_id=1, source_target_pairs={{0,224},{32,0},{64,32},{96,64},{128,96},{160,128},{192,160},{224,1... | collective-permute-start | bytes 786440 | tf_op jit(solution)/shard_map/ppermute | solution.py:273
  74.1 0.0 collective-permute-start.12
  74.1 12.0 %collective-permute-done.11.refs_4_ = bf16[128,1024]{1,0:T(8,128)(2,1)S(1)} collective-permute-done((bf16[128,1024]{1,0:T(8,128)(2,1)S(1)}, bf16[128,1024]{1,0:T(8,128)(2,1)S(1)}, u32[]{:S(2)}, u32[]{:S(2)}) %collective-permute-start.11) | collective-permute-done | bytes 262176 | tf_op jit(solution)/shard_map/ppermute | solution.py:273
  86.1 1.5 %collective-permute-start.13 = (bf16[128,1024]{1,0:T(8,128)(2,1)S(1)}, bf16[128,1024]{1,0:T(8,128)(2,1)S(1)}, u32[]{:S(2)}, u32[]{:S(2)}) collective-permute-start(bf16[128,1024]{1,0:T(8,128)(2,1)S(1)} %collective-permute-done.11.refs_4_), channel_id=1, source_target_pairs={{0,224},{32,0},{64,32},{96,64},{128,96},{160,128},{192,160},{224,1... | collective-permute-start | bytes 786440 | tf_op jit(solution)/shard_map/ppermute | solution.py:273
  87.6 0.5 collective-permute-start.14
  88.1 4.3 %collective-permute-done.13.refs_6_ = bf16[128,1024]{1,0:T(8,128)(2,1)S(1)} collective-permute-done((bf16[128,1024]{1,0:T(8,128)(2,1)S(1)}, bf16[128,1024]{1,0:T(8,128)(2,1)S(1)}, u32[]{:S(2)}, u32[]{:S(2)}) %collective-permute-start.13) | collective-permute-done | bytes 262176 | tf_op jit(solution)/shard_map/ppermute | solution.py:273
  92.5 2.7 %collective-permute-done.14.refs_7_ = bf16[128,1024]{1,0:T(8,128)(2,1)S(1)} collective-permute-done((bf16[128,1024]{1,0:T(8,128)(2,1)S(1)}, bf16[128,1024]{1,0:T(8,128)(2,1)S(1)}, u32[]{:S(2)}, u32[]{:S(2)}) %collective-permute-start.14) | collective-permute-done | bytes 262176 | tf_op jit(solution)/shard_map/ppermute | solution.py:273
  95.2 2.1 %normed.1.nt_ref = bf16[1024,1024]{1,0:T(8,128)(2,1)S(1)} custom-call(bf16[128,1024]{1,0:T(8,128)(2,1)} %bitcast.x_ref.refs_0_, bf16[128,1024]{1,0:T(8,128)(2,1)S(1)} %collective-permute-done.8.refs_1_, bf16[128,1024]{1,0:T(8,128)(2,1)S(1)} %collective-permute-done.9.refs_2_, bf16[128,1024]{1,0:T(8,128)(2,1)S(1)} %collective-permute-done.10.refs_3_, ...), custom_call_target="tpu_custom_call" | custom-call | tf_op jit(solution)/shard_map/normed/pallas_call | solution.py:242
  97.4 1.3 copy-done.3
  98.7 1.6 %copy-done.4 = bf16[1024,1024]{1,0:T(8,128)(2,1)S(1)} copy-done((bf16[1024,1024]{1,0:T(8,128)(2,1)S(1)}, bf16[1024,1024]{1,0:T(8,128)(2,1)}, u32[]{:S(2)}) %copy-start.4) | copy-done | bytes 2097176
  100.3 1.5 %weight.1 = bf16[8,400,128]{2,1,0:T(8,128)(2,1)S(1)} custom-call(bf16[8,208,128]{2,1,0:T(8,128)(2,1)S(1)} %all-to-all-done.g_ref, bf16[1024,1024]{1,0:T(8,128)(2,1)S(1)} %copy-done.4), custom_call_target="tpu_custom_call" | custom-call | tf_op jit(solution)/shard_map/weight/pallas_call | solution.py:242
  101.8 16.1 %all_to_all.15.in_ref = bf16[8,400,128]{2,1,0:T(8,128)(2,1)S(1)} all-to-all(bf16[8,400,128]{2,1,0:T(8,128)(2,1)S(1)} %weight.1), channel_id=1, replica_groups=mesh['dp'=8,'pipe'=4,'seq'=8] {'seq'}, dimensions={0} | all-to-all | bytes 1638400 | tf_op jit(solution)/shard_map/all_to_all | solution.py:339
  117.9 0.8 sum.1
  118.7 7.0 %all-to-all-start.2 = ((bf16[8,64,128]{2,1,0:T(8,128)(2,1)}), bf16[8,64,128]{2,1,0:T(8,128)(2,1)S(1)}, u32[]{:S(2)}, u32[]{:S(2)}) async-start(bf16[8,64,128]{2,1,0:T(8,128)(2,1)} %sum.1), calls=%async_computation.2 | async-start | bytes 262144 | tf_op jit(solution)/shard_map/all_to_all | solution.py:341
  125.7 2.8 %copy-done.2 = bf16[1,3072,1024]{2,1,0:T(8,128)(2,1)S(1)} copy-done((bf16[1,3072,1024]{2,1,0:T(8,128)(2,1)S(1)}, bf16[1,3072,1024]{2,1,0:T(8,128)(2,1)}, u32[]{:S(2)}) %copy-start.2) | copy-done | bytes 6291480
  128.4 4.2 %last.1 = bf16[128,1024]{1,0:T(8,128)(2,1)} custom-call(bf16[128,1024]{1,0:T(8,128)(2,1)S(1)} %collective-permute-done.6.main_ref, bf16[64,1024]{1,0:T(8,128)(2,1)S(1)} %collective-permute-done.7.halo_ref, f32[192,1024]{1,0:T(8,128)S(1)} %get-tuple-element.15.top_ref, f32[192,1024]{1,0:T(8,128)S(1)} %get-tuple-element.16.gp_ref, ...), custom_call_target="tpu_custom_call" | custom-call | tf_op jit(solution)/shard_map/last/pallas_call | solution.py:242
  132.6 2.2 %all-to-all-done.2.in_ref = bf16[8,64,128]{2,1,0:T(8,128)(2,1)S(1)} async-done(((bf16[8,64,128]{2,1,0:T(8,128)(2,1)}), bf16[8,64,128]{2,1,0:T(8,128)(2,1)S(1)}, u32[]{:S(2)}, u32[]{:S(2)}) %all-to-all-start.2) | async-done | bytes 131104 | tf_op jit(solution)/shard_map/all_to_all | solution.py:341
  134.9 0.7 place.1
  (18 shorter events, 0.1 us)
Async XLA Ops:
  3.6 5.3 %collective-permute-start.1 = (bf16[80,1024]{1,0:T(8,128)(2,1)S(1)}, bf16[80,1024]{1,0:T(8,128)(2,1)S(1)}, u32[]{:S(2)}, u32[]{:S(2)}) collective-permute-start(bf16[80,1024]{1,0:T(8,128)(2,1)S(1)} %pad_maximum_fusion.own_ref), channel_id=1, source_target_pairs={{1,0},{2,1},{3,2},{4,3},{5,4},{6,5},{7,6},{9,8},{10,9},{11,10},{12... | collective-permute-start | bytes 491528 | tf_op jit(solution)/shard_map/ppermute | solution.py:269
  4.9 4.0 %collective-permute-start = (bf16[64,1024]{1,0:T(8,128)(2,1)S(1)}, bf16[64,1024]{1,0:T(8,128)(2,1)S(1)}, u32[]{:S(2)}, u32[]{:S(2)}) collective-permute-start(bf16[64,1024]{1,0:T(8,128)(2,1)S(1)} %get-tuple-element.24), channel_id=1, source_target_pairs={{0,1},{1,2},{2,3},{3,4},{4,5},{5,6},{6,7},{8,9},{9,10},{10,11},{11... | collective-permute-start | bytes 393224 | tf_op jit(solution)/shard_map/ppermute | solution.py:270
  8.9 2.8 %copy-start = (bf16[1,3072,1024]{2,1,0:T(8,128)(2,1)S(1)}, bf16[1,3072,1024]{2,1,0:T(8,128)(2,1)}, u32[]{:S(2)}) copy-start(bf16[1,3072,1024]{2,1,0:T(8,128)(2,1)} %param.13) | copy-start | bytes 18874372
  11.7 0.9 copy-start.5
  12.6 0.7 copy-start.6
  13.3 18.0 %copy-start.1 = (bf16[1,3072,1024]{2,1,0:T(8,128)(2,1)S(1)}, bf16[1,3072,1024]{2,1,0:T(8,128)(2,1)}, u32[]{:S(2)}) copy-start(bf16[1,3072,1024]{2,1,0:T(8,128)(2,1)} %param.13) | copy-start | bytes 18874372
  19.6 11.8 %collective-permute-start.2 = (bf16[128,1024]{1,0:T(8,128)(2,1)S(1)}, bf16[128,1024]{1,0:T(8,128)(2,1)S(1)}, u32[]{:S(2)}, u32[]{:S(2)}) collective-permute-start(bf16[128,1024]{1,0:T(8,128)(2,1)S(1)} %get-tuple-element.13), channel_id=1, source_target_pairs={{8,0},{16,8},{24,16},{9,1},{17,9},{25,17},{10,2},{18,10},{26,18},{... | collective-permute-start | bytes 786440 | tf_op jit(solution)/shard_map/ppermute | solution.py:276
  23.6 7.7 %collective-permute-start.3 = (bf16[16,1024]{1,0:T(8,128)(2,1)S(1)}, bf16[16,1024]{1,0:T(8,128)(2,1)S(1)}, u32[]{:S(2)}, u32[]{:S(2)}) collective-permute-start(bf16[16,1024]{1,0:T(8,128)(2,1)S(1)} %get-tuple-element.14), channel_id=1, source_target_pairs={{9,0},{10,1},{11,2},{12,3},{13,4},{14,5},{15,6},{17,8},{18,9},{19,... | collective-permute-start | bytes 98312 | tf_op jit(solution)/shard_map/ppermute | solution.py:286
  34.8 27.0 %copy-start.7 = (s32[1,128]{1,0:T(1,128)S(1)}, s32[1,128]{1,0:T(1,128)}, u32[]{:S(2)}) copy-start(s32[1,128]{1,0:T(1,128)} %ids_ref.1) | copy-start | bytes 1540
  34.9 11.3 %collective-permute-start.4 = (bf16[128,1024]{1,0:T(8,128)(2,1)S(1)}, bf16[128,1024]{1,0:T(8,128)(2,1)S(1)}, u32[]{:S(2)}, u32[]{:S(2)}) collective-permute-start(bf16[128,1024]{1,0:T(8,128)(2,1)S(1)} %get-tuple-element.17), channel_id=1, source_target_pairs={{8,0},{16,8},{24,16},{9,1},{17,9},{25,17},{10,2},{18,10},{26,18},{... | collective-permute-start | bytes 786440 | tf_op jit(solution)/shard_map/ppermute | solution.py:276
  38.9 7.0 %collective-permute-start.5 = (bf16[32,1024]{1,0:T(8,128)(2,1)S(1)}, bf16[32,1024]{1,0:T(8,128)(2,1)S(1)}, u32[]{:S(2)}, u32[]{:S(2)}) collective-permute-start(bf16[32,1024]{1,0:T(8,128)(2,1)S(1)} %get-tuple-element.18), channel_id=1, source_target_pairs={{9,0},{10,1},{11,2},{12,3},{13,4},{14,5},{15,6},{17,8},{18,9},{19,... | collective-permute-start | bytes 196616 | tf_op jit(solution)/shard_map/ppermute | solution.py:286
  40.2 19.0 %collective-permute-start.8 = (bf16[128,1024]{1,0:T(8,128)(2,1)}, bf16[128,1024]{1,0:T(8,128)(2,1)S(1)}, u32[]{:S(2)}, u32[]{:S(2)}) collective-permute-start(bf16[128,1024]{1,0:T(8,128)(2,1)} %bitcast.x_ref.refs_0_), channel_id=1, source_target_pairs={{0,32},{32,64},{64,96},{96,128},{128,160},{160,192},{192,224},{224... | collective-permute-start | bytes 786440 | tf_op jit(solution)/shard_map/ppermute | solution.py:273
  49.7 12.2 %collective-permute-start.6 = (bf16[128,1024]{1,0:T(8,128)(2,1)S(1)}, bf16[128,1024]{1,0:T(8,128)(2,1)S(1)}, u32[]{:S(2)}, u32[]{:S(2)}) collective-permute-start(bf16[128,1024]{1,0:T(8,128)(2,1)S(1)} %get-tuple-element.19), channel_id=1, source_target_pairs={{8,0},{16,8},{24,16},{9,1},{17,9},{25,17},{10,2},{18,10},{26,18},{... | collective-permute-start | bytes 786440 | tf_op jit(solution)/shard_map/ppermute | solution.py:276
  53.7 8.1 %collective-permute-start.7 = (bf16[64,1024]{1,0:T(8,128)(2,1)S(1)}, bf16[64,1024]{1,0:T(8,128)(2,1)S(1)}, u32[]{:S(2)}, u32[]{:S(2)}) collective-permute-start(bf16[64,1024]{1,0:T(8,128)(2,1)S(1)} %get-tuple-element.20), channel_id=1, source_target_pairs={{9,0},{10,1},{11,2},{12,3},{13,4},{14,5},{15,6},{17,8},{18,9},{19,... | collective-permute-start | bytes 393224 | tf_op jit(solution)/shard_map/ppermute | solution.py:286
  55.0 15.9 %collective-permute-start.9 = (bf16[128,1024]{1,0:T(8,128)(2,1)}, bf16[128,1024]{1,0:T(8,128)(2,1)S(1)}, u32[]{:S(2)}, u32[]{:S(2)}) collective-permute-start(bf16[128,1024]{1,0:T(8,128)(2,1)} %bitcast.x_ref.refs_0_), channel_id=1, source_target_pairs={{0,224},{32,0},{64,32},{96,64},{128,96},{160,128},{192,160},{224,1... | collective-permute-start | bytes 786440 | tf_op jit(solution)/shard_map/ppermute | solution.py:273
  59.2 14.9 %collective-permute-start.10 = (bf16[128,1024]{1,0:T(8,128)(2,1)S(1)}, bf16[128,1024]{1,0:T(8,128)(2,1)S(1)}, u32[]{:S(2)}, u32[]{:S(2)}) collective-permute-start(bf16[128,1024]{1,0:T(8,128)(2,1)S(1)} %collective-permute-done.8.refs_1_), channel_id=1, source_target_pairs={{0,32},{32,64},{64,96},{96,128},{128,160},{160,192},{192,224},{224... | collective-permute-start | bytes 786440 | tf_op jit(solution)/shard_map/ppermute | solution.py:273
  62.7 36.0 %all-to-all-start = ((bf16[8,208,128]{2,1,0:T(8,128)(2,1)}), bf16[8,208,128]{2,1,0:T(8,128)(2,1)S(1)}, u32[]{:S(2)}, u32[]{:S(2)}) async-start(bf16[8,208,128]{2,1,0:T(8,128)(2,1)} %pack.1), calls=%async_computation | async-start | bytes 851968 | tf_op jit(solution)/shard_map/all_to_all | solution.py:324
  70.9 15.2 %collective-permute-start.11 = (bf16[128,1024]{1,0:T(8,128)(2,1)S(1)}, bf16[128,1024]{1,0:T(8,128)(2,1)S(1)}, u32[]{:S(2)}, u32[]{:S(2)}) collective-permute-start(bf16[128,1024]{1,0:T(8,128)(2,1)S(1)} %collective-permute-done.9.refs_2_), channel_id=1, source_target_pairs={{0,224},{32,0},{64,32},{96,64},{128,96},{160,128},{192,160},{224,1... | collective-permute-start | bytes 786440 | tf_op jit(solution)/shard_map/ppermute | solution.py:273
  74.1 13.5 %collective-permute-start.12 = (bf16[128,1024]{1,0:T(8,128)(2,1)S(1)}, bf16[128,1024]{1,0:T(8,128)(2,1)S(1)}, u32[]{:S(2)}, u32[]{:S(2)}) collective-permute-start(bf16[128,1024]{1,0:T(8,128)(2,1)S(1)} %collective-permute-done.10.refs_3_), channel_id=1, source_target_pairs={{0,32},{32,64},{64,96},{96,128},{128,160},{160,192},{192,224},{224... | collective-permute-start | bytes 786440 | tf_op jit(solution)/shard_map/ppermute | solution.py:273
  86.1 6.4 %collective-permute-start.13 = (bf16[128,1024]{1,0:T(8,128)(2,1)S(1)}, bf16[128,1024]{1,0:T(8,128)(2,1)S(1)}, u32[]{:S(2)}, u32[]{:S(2)}) collective-permute-start(bf16[128,1024]{1,0:T(8,128)(2,1)S(1)} %collective-permute-done.11.refs_4_), channel_id=1, source_target_pairs={{0,224},{32,0},{64,32},{96,64},{128,96},{160,128},{192,160},{224,1... | collective-permute-start | bytes 786440 | tf_op jit(solution)/shard_map/ppermute | solution.py:273
  87.6 7.6 %collective-permute-start.14 = (bf16[128,1024]{1,0:T(8,128)(2,1)S(1)}, bf16[128,1024]{1,0:T(8,128)(2,1)S(1)}, u32[]{:S(2)}, u32[]{:S(2)}) collective-permute-start(bf16[128,1024]{1,0:T(8,128)(2,1)S(1)} %collective-permute-done.12.refs_5_), channel_id=1, source_target_pairs={{0,32},{32,64},{64,96},{96,128},{128,160},{160,192},{192,224},{224... | collective-permute-start | bytes 786440 | tf_op jit(solution)/shard_map/ppermute | solution.py:273
  97.4 1.3 copy-start.3
  98.7 1.6 %copy-start.4 = (bf16[1024,1024]{1,0:T(8,128)(2,1)S(1)}, bf16[1024,1024]{1,0:T(8,128)(2,1)}, u32[]{:S(2)}) copy-start(bf16[1024,1024]{1,0:T(8,128)(2,1)} %copy-done.3) | copy-start | bytes 6291460
  118.7 16.2 %all-to-all-start.2 = ((bf16[8,64,128]{2,1,0:T(8,128)(2,1)}), bf16[8,64,128]{2,1,0:T(8,128)(2,1)S(1)}, u32[]{:S(2)}, u32[]{:S(2)}) async-start(bf16[8,64,128]{2,1,0:T(8,128)(2,1)} %sum.1), calls=%async_computation.2 | async-start | bytes 262144 | tf_op jit(solution)/shard_map/all_to_all | solution.py:341
  125.6 2.8 %copy-start.2 = (bf16[1,3072,1024]{2,1,0:T(8,128)(2,1)S(1)}, bf16[1,3072,1024]{2,1,0:T(8,128)(2,1)}, u32[]{:S(2)}) copy-start(bf16[1,3072,1024]{2,1,0:T(8,128)(2,1)} %param.13) | copy-start | bytes 18874372
